TPU v7x, 256 devices: a whole 4x4x8 slice. The times are simulated.
256 devices in a mesh: width: 16 (over z, x_hi), chan: 16 (over y, x_lo, core).
Axes of the slice: x: 4 (x_hi: 2, x_lo: 2; x = x_hi * 2 + x_lo), y: 4, z: 8, core: 2. Of those that a mesh axis runs over, the one named last changes fastest.
Arguments:
- activations: bfloat16 [512, 2, 12288], P('chan', None, 'width'), may hold values from -6 to 6
- filters: bfloat16 [512, 3, 3, 512], P('chan'), may hold values from -0.125 to 0.125
- cotangent: bfloat16 [512, 2, 12288], P('chan', None, 'width'), may hold values from -6 to 6
Outputs:
- conv_output: bfloat16 [512, 2, 12288], P('chan', None, 'width')
- input_grad: bfloat16 [512, 2, 12288], P('chan', None, 'width')
- filter_grad: float32 [512, 3, 3, 512], P('chan')
All inputs are finite; a program needn't handle non-finite values.
Results may differ from a plain program's by a relative error of at most 0.001.
Values may be sent and summed in bfloat16 or wider, within the bound.
A program may use at most 128 MiB of HBM per device.

v0:
```python
import math

import jax
import jax.numpy as jnp
from jax import lax
from jax.sharding import PartitionSpec as P


def padded_2(shard, sides, width):
    for axis, dim in sides:
        devices, length = (lax.axis_size(axis), shard.shape[dim])
        up = [(i, (i + 1) % devices) for i in range(devices - 1)]
        down = [(j, i) for i, j in up]
        last = lax.slice_in_dim(shard, length - width, length, axis=dim)
        leading = lax.slice_in_dim(shard, 0, width, axis=dim)
        before = lax.ppermute(last, axis, up)
        after = lax.ppermute(leading, axis, down)
        shard = jnp.concatenate([before, shard, after], axis=dim)
    return shard


def pad_rows(field):
    return jnp.pad(field, ((0, 0), (1, 1), (0, 0)))


def stack_taps(padded, rows, cols, flipped):
    pieces = []
    for tap_row in range(3):
        for tap_col in range(3):
            first_row = 2 - tap_row if flipped else tap_row
            first_col = 2 - tap_col if flipped else tap_col
            pieces.append(
                padded[:, first_row : first_row + rows, first_col : first_col + cols].reshape(
                    padded.shape[0], rows * cols
                )
            )
    return jnp.concatenate(pieces, 0)


def tap_major(block):
    number_in = block.shape[0]
    number_out = block.shape[3]
    return jnp.transpose(block, (1, 2, 0, 3)).reshape(9 * number_in, number_out)


def body(activations, filters, cotangent):
    cin_dev, rows, cols = activations.shape
    cout_dev = cotangent.shape[0]
    edged = padded_2(activations, (("width", 2),), 1)
    source_stack = stack_taps(pad_rows(edged), rows, cols, False)
    block = tap_major(filters)
    summed = lax.dot_general(
        block, source_stack, (((0,), (0,)), ((), ())), preferred_element_type=jnp.float32
    )
    forward = lax.psum_scatter(
        summed.reshape(cout_dev * lax.axis_size("chan"), rows, cols),
        "chan",
        scatter_dimension=0,
        tiled=True,
    )
    conv_output = forward.astype(jnp.bfloat16)
    grad_edged = padded_2(cotangent, (("width", 2),), 1)
    shards = lax.all_gather(grad_edged, "chan", axis=0, tiled=True)
    number_rows = shards.shape[0]
    block = filters.reshape(cin_dev, 9 * number_rows)
    grad_stack = stack_taps(pad_rows(shards), rows, cols, True)
    input_sum = jnp.dot(block, grad_stack, preferred_element_type=jnp.float32)
    interior = shards[:, :, 1:-1].reshape(number_rows, rows * cols)
    tap_grads = lax.dot_general(
        source_stack, interior, (((1,), (1,)), ((), ())), preferred_element_type=jnp.float32
    )
    tap_grads = jnp.transpose(tap_grads.reshape(3, 3, cin_dev, number_rows), (2, 0, 1, 3))
    filter_sum = tap_grads
    input_sum, filter_sum = (input_sum, filter_sum)
    filter_total = lax.psum(filter_sum, "width")
    factor = 1.0 / math.sqrt(rows * cols * lax.axis_size("width"))
    input_grad = input_sum.reshape(cin_dev, rows, cols).astype(jnp.bfloat16)
    return (conv_output, input_grad, filter_total * factor)


def solution(mesh):
    in_specs = (P("chan", None, "width"), P("chan", None, None, None), P("chan", None, "width"))
    out_specs = (P("chan", None, "width"), P("chan", None, "width"), P("chan", None, None, None))
    return jax.shard_map(body, mesh=mesh, in_specs=in_specs, out_specs=out_specs, check_vma=False)
```

profile of v0, /device:TPU:4, one launch (start us, length us, event | category | flops | bytes accessed | tf_op | source)
XLA Modules:
  0.0 343.5 jit_solution(17910656039230067917)
XLA Ops:
  8.1 3.8 %collective-permute-start.2 = (bf16[32,2,1]{2,1,0:T(2,128)(2,1)S(1)}, bf16[32,2,1]{2,1,0:T(2,128)(2,1)S(1)}, u32[]{:S(2)}, u32[]{:S(2)}) collective-permute-start(bf16[32,2,1]{2,1,0:T(2,128)(2,1)S(1)} %get-tuple-element.18), channel_id=1, source_target_pairs={{0,16},{16,32},{32,48},{48,64},{64,80},{80,96},{96,112},{112,128},... | collective-permute-start | bytes 392 | tf_op jit(solution)/shard_map/ppermute | solution.py:16
  11.9 3.6 %collective-permute-start.3 = (bf16[32,2,1]{2,1,0:T(2,128)(2,1)S(1)}, bf16[32,2,1]{2,1,0:T(2,128)(2,1)S(1)}, u32[]{:S(2)}, u32[]{:S(2)}) collective-permute-start(bf16[32,2,1]{2,1,0:T(2,128)(2,1)S(1)} %get-tuple-element.19), channel_id=1, source_target_pairs={{16,0},{32,16},{48,32},{64,48},{80,64},{96,80},{112,96},{128,112},... | collective-permute-start | bytes 392 | tf_op jit(solution)/shard_map/ppermute | solution.py:17
  16.3 4.7 %collective-permute-start = (bf16[32,2,1]{2,1,0:T(2,128)(2,1)S(1)}, bf16[32,2,1]{2,1,0:T(2,128)(2,1)S(1)}, u32[]{:S(2)}, u32[]{:S(2)}) collective-permute-start(bf16[32,2,1]{2,1,0:T(2,128)(2,1)S(1)} %get-tuple-element.22), channel_id=1, source_target_pairs={{0,16},{16,32},{32,48},{48,64},{64,80},{80,96},{96,112},{112,128},... | collective-permute-start | bytes 392 | tf_op jit(solution)/shard_map/ppermute | solution.py:16
  21.0 2.7 collective-permute-start.1
  27.6 1.4 collective-permute-done.1
  32.0 3.5 %copy.9 = f32[512,2,768]{2,1,0:T(2,128)} copy(f32[512,2,768]{0,2,1:T(8,128)S(1)} %bitcast.58) | data formatting | bytes 6291456 | tf_op jit(solution)/shard_map/reshape | solution.py:56
  35.5 88.1 %all-reduce.7 = bf16[512,2,768]{2,1,0:T(2,128)(2,1)S(1)} all-reduce(f32[512,2,768]{2,1,0:T(2,128)} %copy.9), channel_id=2, replica_groups=mesh['width'=16,'chan'=16] {'chan'}, use_global_device_ids=true, to_apply=%region_0.1.clone | all-reduce | flops 786432 | bytes 4718592
  124.3 33.4 %pad_slice_fusion = (bf16[512,2,768]{2,1,0:T(2,128)(2,1)}, bf16[512,2,768]{2,1,0:T(2,128)(2,1)S(1)}, bf16[512,2,768]{2,1,0:T(2,128)(2,1)S(1)}, bf16[512,2,768]{2...) fusion(bf16[512,2,770]{2,1,0:T(2,128)(2,1)} %all-gather.2.clone, ...), kind=kLoop, calls=%fused_computation | loop fusion | bytes 20709376 | tf_op jit(solution)/shard_map/slice | solution.py:33
  159.2 1.4 copy.22
  160.7 1.4 copy.23
  162.1 1.4 copy.24
  163.5 1.9 reshape.95
  165.4 1.4 copy.25
  167.3 1.4 copy.26
  169.2 1.4 copy.27
  173.7 1.5 fusion.3
  175.2 2.8 constant_dynamic-update-slice_fusion.16
  179.9 1.3 constant_dynamic-update-slice_fusion.14
  183.9 1.3 constant_dynamic-update-slice_fusion.12
  187.1 1.3 constant_dynamic-update-slice_fusion.10
  188.4 1.3 constant_dynamic-update-slice_fusion.9
  189.7 7.5 %fusion = bf16[32,1536]{1,0:T(8,128)(2,1)S(1)} fusion(bf16[32,4608]{1,0:T(8,128)(2,1)S(1)} %reshape.94, bf16[4608,1536]{1,0:T(8,128)(2,1)} %constant_dynamic-update-slice_fusion.9), kind=kOutput, calls=%fused_computation.7 | convolution fusion | flops 453033984 | bytes 14548992 | tf_op jit(solution)/shard_map/dot_general | solution.py:67
  197.9 136.9 %all-reduce.6.cloned.1.call-done = f32[32,3,3,512]{3,0,2,1:T(8,128)} async-done(((f32[32,3,3,512]{3,0,2,1:T(8,128)}), f32[32,3,3,512]{3,0,2,1:T(8,128)}) %all-reduce.6.cloned.1.call-update) | async-done | bytes 589840 | tf_op jit(solution)/shard_map/psum | solution.py:75
  334.8 1.9 broadcast_multiply_fusion
  (75 shorter events, 21.3 us)
Async XLA Ops:
  7.2 18.2 %copy-start.14 = (u32[256]{0:T(256)S(1)}, u32[256]{0:T(256)}, u32[]{:S(2)}) copy-start(u32[256]{0:T(256)} %constant.11) | copy-start | bytes 3076
  7.2 19.4 %copy-start.13 = (bf16[32,2,768]{2,1,0:T(2,128)(2,1)S(1)}, bf16[32,2,768]{2,1,0:T(2,128)(2,1)}, u32[]{:S(2)}) copy-start(bf16[32,2,768]{2,1,0:T(2,128)(2,1)} %param.5) | copy-start | bytes 294916
  7.2 18.1 %copy-start.12 = (bf16[32,2,768]{2,1,0:T(2,128)(2,1)S(1)}, bf16[32,2,768]{2,1,0:T(2,128)(2,1)}, u32[]{:S(2)}) copy-start(bf16[32,2,768]{2,1,0:T(2,128)(2,1)} %param.3) | copy-start | bytes 294916
  7.2 117.1 %all-gather.2.cloned.1.call-start = ((), (), s32[]{:S(2)}) async-start(), calls=%async_computation | async-start | bytes 1949696 | tf_op jit(solution)/shard_map/all_gather | solution.py:63
  8.1 18.5 %collective-permute-start.2 = (bf16[32,2,1]{2,1,0:T(2,128)(2,1)S(1)}, bf16[32,2,1]{2,1,0:T(2,128)(2,1)S(1)}, u32[]{:S(2)}, u32[]{:S(2)}) collective-permute-start(bf16[32,2,1]{2,1,0:T(2,128)(2,1)S(1)} %get-tuple-element.18), channel_id=1, source_target_pairs={{0,16},{16,32},{32,48},{48,64},{64,80},{80,96},{96,112},{112,128},... | collective-permute-start | bytes 392 | tf_op jit(solution)/shard_map/ppermute | solution.py:16
  11.9 14.7 %collective-permute-start.3 = (bf16[32,2,1]{2,1,0:T(2,128)(2,1)S(1)}, bf16[32,2,1]{2,1,0:T(2,128)(2,1)S(1)}, u32[]{:S(2)}, u32[]{:S(2)}) collective-permute-start(bf16[32,2,1]{2,1,0:T(2,128)(2,1)S(1)} %get-tuple-element.19), channel_id=1, source_target_pairs={{16,0},{32,16},{48,32},{64,48},{80,64},{96,80},{112,96},{128,112},... | collective-permute-start | bytes 392 | tf_op jit(solution)/shard_map/ppermute | solution.py:17
  16.3 11.3 %collective-permute-start = (bf16[32,2,1]{2,1,0:T(2,128)(2,1)S(1)}, bf16[32,2,1]{2,1,0:T(2,128)(2,1)S(1)}, u32[]{:S(2)}, u32[]{:S(2)}) collective-permute-start(bf16[32,2,1]{2,1,0:T(2,128)(2,1)S(1)} %get-tuple-element.22), channel_id=1, source_target_pairs={{0,16},{16,32},{32,48},{48,64},{64,80},{80,96},{96,112},{112,128},... | collective-permute-start | bytes 392 | tf_op jit(solution)/shard_map/ppermute | solution.py:16
  21.0 8.0 %collective-permute-start.1 = (bf16[32,2,1]{2,1,0:T(2,128)(2,1)S(1)}, bf16[32,2,1]{2,1,0:T(2,128)(2,1)S(1)}, u32[]{:S(2)}, u32[]{:S(2)}) collective-permute-start(bf16[32,2,1]{2,1,0:T(2,128)(2,1)S(1)} %get-tuple-element.23), channel_id=1, source_target_pairs={{16,0},{32,16},{48,32},{64,48},{80,64},{96,80},{112,96},{128,112},... | collective-permute-start | bytes 392 | tf_op jit(solution)/shard_map/ppermute | solution.py:17
  27.5 307.3 %all-reduce.6.cloned.1.call-start = ((), (), s32[]{:S(2)}) async-start(), calls=%async_computation.1 | async-start | bytes 1179648 | tf_op jit(solution)/shard_map/psum | solution.py:75
  30.1 1.0 copy-start.11
  30.7 1.4 copy-start.8
  165.4 1.9 copy-start.7
  167.3 1.9 copy-start.6
  170.6 1.4 copy-start.5
  172.0 1.2 copy-start.9
  172.0 1.7 copy-start.10
  175.2 2.8 copy-start.4
  178.0 2.0 copy-start.2
  179.9 2.0 copy-start.3
  181.9 2.0 copy-start.1
  183.9 2.0 copy-start
Sparse Core Ops, SparseCore 0:
  27.6 44.5 all-gather.1
  175.3 159.4 all-reduce.5
where the time goes:
time: 345 us; the launch traced here: 344 us
  waiting for transfers between devices  138 us (40%)
  blocking collectives  88.1 us (26%)
  local copies, waits for them, and re-layouts  73.8 us (21%)
  between operations  15.1 us (4%)
  starting transfers between devices  14.8 us (4%)
  matrix products  10 us (3%)
  other arithmetic  3.53 us (1%)
    psum x1, waiting for transfers between devices, body(): filter_total = lax.psum(filter_sum, 'width')  137 us
    unnamed x1, blocking collectives  88.1 us
    slice x2, local copies, waits for them, and re-layouts, stack_taps(): padded[:, first_row:first_row + rows, first_col:first_col + cols]  34 us
    unnamed x66, local copies, waits for them, and re-layouts  29.6 us
    ppermute x2, starting transfers between devices, padded_2(): before = lax.ppermute(last, axis, up)  8.44 us
    dot_general x1, matrix products, body(): input_sum = jnp.dot(block, grad_stack, preferred_element_type=jnp.float32)  7.55 us
  transfers between devices with their start and end apart: 6, of which 2 were waited for; matrix products, arithmetic and copies ran while one was open for 9% of the time, Pallas kernels for 0%

commit v1 on v0

v1 whole, which is shorter than its diff:
```python
import math

import jax
import jax.numpy as jnp
from jax import lax
from jax.experimental import pallas as pl
from jax.experimental.pallas import tpu as pltpu
from jax.sharding import PartitionSpec as P

MESH = pl.DeviceIdType.MESH
BF16 = jnp.bfloat16
F32 = jnp.float32

Y_UP, Y_DOWN, ACROSS, CORE = "up", "down", "across", "core"


def arrived(piece, way):
    h, dy, dx, dc = piece
    if way == Y_UP:
        return (h, (dy - 1) % 4, dx, dc)
    if way == Y_DOWN:
        return (h, (dy + 1) % 4, dx, dc)
    if way == ACROSS:
        return (h, dy, 1 - dx, dc)
    return (h, dy, dx, 1 - dc)


def gather_plan(relay):
    first = [
        ((0, 0, 0, 0), Y_UP),
        ((0, 0, 0, 0), Y_DOWN),
        ((1, 0, 0, 0), ACROSS),
        ((1, 0, 0, 0), Y_UP),
        ((1, 0, 0, 0), Y_DOWN),
        ((0, 0, 0, 0), ACROSS),
        ((0, 0, 0, 0), CORE),
        ((1, 0, 0, 0), CORE),
    ]
    up = [Y_UP] if relay == Y_UP else []
    down = [Y_DOWN] if relay == Y_DOWN else []
    stages = [
        [(None, first)],
        [
            ((1, 0, 1, 0), [Y_UP, Y_DOWN, CORE]),
            ((0, 3, 0, 0), up + [ACROSS, CORE]),
            ((0, 1, 0, 0), down + [ACROSS, CORE]),
            ((1, 3, 0, 0), [Y_UP, CORE]),
            ((1, 1, 0, 0), [CORE]),
            ((0, 0, 1, 0), [CORE]),
        ],
        [
            ((1, 1, 1, 0), [Y_DOWN, CORE]),
            ((1, 3, 1, 0), [CORE]),
            ((0, 2, 0, 0), [ACROSS, CORE]),
            ((0, 3, 1, 0), [CORE]),
            ((0, 1, 1, 0), [CORE]),
            ((1, 2, 0, 0), [CORE]),
        ],
        [
            ((1, 2, 1, 0), [CORE]),
            ((0, 2, 1, 0), [CORE]),
        ],
    ]
    plan = []
    for stage in stages:
        steps = []
        for piece, sends in stage:
            if piece is not None:
                sends = [(piece, way) for way in sends]
            steps.append((piece, sends))
        plan.append(steps)
    return plan


def message_ids(plan):
    brings, number = {}, {}
    for steps in plan:
        for _, sends in steps:
            for piece, way in sends:
                number[(piece, way)] = len(number)
                brings[arrived(piece, way)] = number[(piece, way)]
    return brings, number


PLANS = [gather_plan(Y_UP), gather_plan(Y_DOWN)]
N_MSG = 30


def kernel(
    n_width,
    factor,
    x_ref,
    g_ref,
    f_ref,
    conv_ref,
    grad_ref,
    filt_ref,
    x_all,
    g_all,
    f_all,
    f_msg,
    halo,
    xs,
    part,
    rs_buf,
    e_out,
    e_in,
    y_buf,
    gat_send,
    gat_recv,
    f_send,
    f_recv,
    halo_send,
    halo_recv,
    rs_send,
    rs_recv,
    ag_send,
    ag_recv,
    e_send,
    e_recv,
):
    w = lax.axis_index("width")
    k = lax.axis_index("chan")
    py = k // 4
    px = (k // 2) % 2
    pc = k % 2
    cols = x_ref.shape[2]
    right = lax.rem(w + 1, n_width)
    left = lax.rem(w + n_width - 1, n_width)

    def chan_of(dy, dx, dc):
        y = lax.rem(py + dy, 4)
        x = 1 - px if dx else px
        c = 1 - pc if dc else pc
        return y * 4 + x * 2 + c

    ways = {
        Y_UP: chan_of(1, 0, 0),
        Y_DOWN: chan_of(3, 0, 0),
        ACROSS: chan_of(0, 1, 0),
        CORE: chan_of(0, 0, 1),
    }

    barrier = pltpu.get_barrier_semaphore()
    for d in range(1, 16):
        pl.semaphore_signal(
            barrier, inc=1, device_id={"chan": lax.rem(k + d, 16)}, device_id_type=MESH
        )
    for d in range(1, n_width):
        pl.semaphore_signal(
            barrier, inc=1, device_id={"width": lax.rem(w + d, n_width)}, device_id_type=MESH
        )

    lane = lax.broadcasted_iota(jnp.int32, (96, 128), 1)

    for tile in range(4):
        parts = [
            f_ref[:, b, :, tile * 128 : tile * 128 + 128].reshape(96, 128).astype(F32)
            for b in range(3)
        ]
        for j in range(4):
            out = jnp.zeros((96, 128), F32)
            for b in range(3):
                moved = parts[b]
                if (b - j) % 4:
                    moved = pltpu.roll(moved, ((b - j) % 4) * 32, 1)
                out = jnp.where(lane // 32 == b, moved, out)
            f_msg[tile * 4 + j] = out.astype(BF16).reshape(3, 32, 128)

    def own_rows(index):
        return pl.ds(pl.multiple_of(index * 32, 32), 32)

    x_all[:, own_rows(k), :] = x_ref[...]
    g_all[:, own_rows(k), :] = g_ref[...]
    f_all[:, own_rows(k), :] = f_msg[k]

    pl.semaphore_wait(barrier, 15 + n_width - 1)

    pending = []

    def start(copy):
        copy.start()
        pending.append(copy)

    arrays = [(g_all, g_ref), (x_all, x_ref)]
    brings_of = [message_ids(plan)[0] for plan in PLANS]
    number_of = [message_ids(plan)[1] for plan in PLANS]

    def piece_ref(which, piece):
        h, dy, dx, dc = piece
        return arrays[which][0].at[h, own_rows(chan_of(dy, dx, dc)), :]

    def gather_send(which, piece, way):
        m = number_of[which][(piece, way)]
        ref = piece_ref(which, piece)
        src = arrays[which][1].at[piece[0]] if piece[1:] == (0, 0, 0) else ref
        start(
            pltpu.make_async_remote_copy(
                src_ref=src,
                dst_ref=ref,
                send_sem=gat_send.at[which, m],
                recv_sem=gat_recv.at[which, m],
                device_id={"chan": ways[way]},
                device_id_type=MESH,
            )
        )

    def gather_wait(which, piece):
        m = brings_of[which][piece]
        ref = piece_ref(which, piece)
        pltpu.make_async_remote_copy(
            src_ref=ref,
            dst_ref=ref,
            send_sem=gat_send.at[which, m],
            recv_sem=gat_recv.at[which, m],
            device_id={"chan": ways[CORE]},
            device_id_type=MESH,
        ).wait_recv()

    def gather_stage(which, number):
        for piece, sends in PLANS[which][number]:
            if piece is not None:
                gather_wait(which, piece)
            for sent, way in sends:
                gather_send(which, sent, way)

    def gather_class(which, dy):
        for dx in range(2):
            for h in range(2):
                gather_wait(which, (h, dy, dx, 1))

    def halo_copy(side, device):
        src = x_ref.at[:, :, cols - 128 : cols] if side == 0 else x_ref.at[:, :, 0:128]
        return pltpu.make_async_remote_copy(
            src_ref=src,
            dst_ref=halo.at[side],
            send_sem=halo_send.at[side],
            recv_sem=halo_recv.at[side],
            device_id={"width": device},
            device_id_type=MESH,
        )

    halo_copies = [halo_copy(0, right), halo_copy(1, left)]
    for copy in halo_copies:
        start(copy)
    gather_stage(0, 0)

    lane64 = lax.broadcasted_iota(jnp.int32, (64, 128), 1)
    mine = x_ref[...].reshape(64, cols)
    xs[64:128, :] = mine
    mine = mine.astype(F32)
    xs[0:64, :] = pltpu.roll(mine, 1, 1).astype(BF16)
    xs[128:192, :] = pltpu.roll(mine, cols - 1, 1).astype(BF16)
    gather_stage(0, 1)
    for copy in halo_copies:
        copy.wait_recv()
    from_left = jnp.where(w > 0, pltpu.roll(halo[0].reshape(64, 128).astype(F32), 1, 1), 0.0)
    xs[0:64, 0:128] = jnp.where(lane64 == 0, from_left, xs[0:64, 0:128].astype(F32)).astype(BF16)
    from_right = jnp.where(
        w < n_width - 1, pltpu.roll(halo[1].reshape(64, 128).astype(F32), 127, 1), 0.0
    )
    xs[128:192, cols - 128 : cols] = jnp.where(
        lane64 == 127, from_right, xs[128:192, cols - 128 : cols].astype(F32)
    ).astype(BF16)

    def rs_copy(block, slot, device):
        return pltpu.make_async_remote_copy(
            src_ref=part.at[block % 4, :, pl.ds(pl.multiple_of(block // 4 * 8, 8), 8), :],
            dst_ref=rs_buf.at[slot],
            send_sem=rs_send.at[block],
            recv_sem=rs_recv.at[slot],
            device_id={"width": device},
            device_id_type=MESH,
        )

    def filter_class(dy):
        group = lax.rem(py + dy, 4)
        rows = pl.ds(pl.multiple_of(group * 128, 128), 128)
        taps = [
            lax.dot_general(
                xs[...], g_all[h, rows, :], (((1,), (1,)), ((), ())), preferred_element_type=F32
            )
            for h in range(2)
        ]
        for b in range(3):
            one, two = slice(b * 64, b * 64 + 32), slice(b * 64 + 32, b * 64 + 64)
            part[group, b] = taps[1][one]
            part[group, 3 + b] = taps[0][one] + taps[1][two]
            part[group, 6 + b] = taps[0][two]
        for c8 in range(4):
            block = c8 * 4 + group

            @pl.when(block != w)
            def _():
                rs_copy(block, w, block).start()

            @pl.when(block == w)
            def _():
                rs_buf[w] = part[group, :, c8 * 8 : c8 * 8 + 8, :]

    def f_copy(d):
        return pltpu.make_async_remote_copy(
            src_ref=f_msg.at[lax.rem(k + d, 16)],
            dst_ref=f_all.at[:, own_rows(k), :],
            send_sem=f_send.at[d],
            recv_sem=f_recv.at[d],
            device_id={"chan": lax.rem(k + d, 16)},
            device_id_type=MESH,
        )

    gather_class(0, 0)
    filter_class(0)
    gather_stage(1, 0)
    gather_stage(0, 2)
    gather_class(0, 3)
    filter_class(3)
    gather_class(0, 1)
    filter_class(1)
    gather_stage(0, 3)
    gather_stage(1, 1)
    for d in range(1, 16):
        start(f_copy(d))
    gather_class(0, 2)
    filter_class(2)
    gather_stage(1, 2)

    lane32 = lax.broadcasted_iota(jnp.int32, (32, cols), 1)

    def edge_copy(which, side, device):
        return pltpu.make_async_remote_copy(
            src_ref=e_out.at[which, side],
            dst_ref=e_in.at[which, side],
            send_sem=e_send.at[which, side],
            recv_sem=e_recv.at[which, side],
            device_id={"width": device},
            device_id_type=MESH,
        )

    def edges_out(which, taps):
        for h in range(2):
            e_out[which, 0, h] = taps[h][0][:, cols - 128 : cols]
            e_out[which, 1, h] = taps[h][2][:, 0:128]
        copies = [edge_copy(which, 0, right), edge_copy(which, 1, left)]
        for copy in copies:
            start(copy)
        for h in range(2):
            moved_right = jnp.where(lane32 == 0, 0.0, pltpu.roll(taps[h][0], 1, 1))
            moved_left = jnp.where(lane32 == cols - 1, 0.0, pltpu.roll(taps[h][2], cols - 1, 1))
            y_buf[which, h] = taps[h][1] + moved_right + moved_left
        return copies

    def edges_in(which, copies, out_ref):
        for copy in copies:
            copy.wait_recv()
        lane128 = lax.broadcasted_iota(jnp.int32, (32, 128), 1)
        for h in range(2):
            came = pltpu.roll(e_in[which, 0, h], 1, 1)
            y_buf[which, h, :, 0:128] += jnp.where((lane128 == 0) & (w > 0), came, 0.0)
            came = pltpu.roll(e_in[which, 1, h], 127, 1)
            y_buf[which, h, :, cols - 128 : cols] += jnp.where(
                (lane128 == 127) & (w < n_width - 1), came, 0.0
            )
            out_ref[h] = y_buf[which, h].astype(BF16)

    sums = None
    for h in range(2):
        block = f_ref[1 - h : 3 - h].reshape(192, f_ref.shape[3])
        term = jnp.dot(block, g_all[h], preferred_element_type=F32)
        sums = term if sums is None else sums + term
    taps = [[sums[h * 96 + b * 32 : h * 96 + b * 32 + 32] for b in (2, 1, 0)] for h in range(2)]
    grad_copies = edges_out(1, taps)

    gather_stage(1, 3)

    for d in range(1, n_width):
        source = lax.rem(w + d, n_width)
        rs_copy(source, source, source).wait_recv()
    total = rs_buf[0]
    for s in range(1, n_width):
        total = total + rs_buf[s]

    def block_ref(index):
        return filt_ref.at[
            :,
            pl.ds(pl.multiple_of(index // 4 * 8, 8), 8),
            pl.ds(pl.multiple_of(index % 4 * 128, 128), 128),
        ]

    filt_ref[
        :,
        pl.ds(pl.multiple_of(w // 4 * 8, 8), 8),
        pl.ds(pl.multiple_of(w % 4 * 128, 128), 128),
    ] = total * factor

    def ag_copy(index, d, device):
        return pltpu.make_async_remote_copy(
            src_ref=block_ref(index),
            dst_ref=block_ref(index),
            send_sem=ag_send.at[d],
            recv_sem=ag_recv.at[d],
            device_id={"width": device},
            device_id_type=MESH,
        )

    for d in range(1, n_width):
        start(ag_copy(w, d, lax.rem(w + d, n_width)))

    for which_dy in range(4):
        gather_class(1, which_dy)
    for d in range(1, 16):
        source = lax.rem(k + 16 - d, 16)
        pltpu.make_async_remote_copy(
            src_ref=f_msg.at[0],
            dst_ref=f_all.at[:, own_rows(source), :],
            send_sem=f_send.at[d],
            recv_sem=f_recv.at[d],
            device_id={"chan": source},
            device_id_type=MESH,
        ).wait_recv()
    depth = f_all.shape[1]
    field = x_all[...].reshape(2 * depth, cols)
    taps = []
    for h in range(2):
        block = f_all[1 - h : 3 - h].reshape(2 * depth, 128)
        sums = lax.dot_general(
            block, field, (((0,), (0,)), ((), ())), preferred_element_type=F32
        )
        taps.append([sums[b * 32 : b * 32 + 32] for b in range(3)])
    conv_copies = edges_out(0, taps)
    edges_in(1, grad_copies, grad_ref)
    edges_in(0, conv_copies, conv_ref)

    for d in range(1, n_width):
        source = lax.rem(w + n_width - d, n_width)
        ag_copy(source, d, source).wait_recv()
    for copy in pending:
        copy.wait_send()
    for d in range(1, n_width):
        block = lax.rem(w + d, n_width)
        rs_copy(block, w, block).wait_send()


def body(activations, filters, cotangent):
    cin_dev, rows, cols = activations.shape
    n_out = filters.shape[3]
    n_width = lax.axis_size("width")
    factor = 1.0 / math.sqrt(rows * cols * n_width)
    x = jnp.transpose(activations, (1, 0, 2))
    g = jnp.transpose(cotangent, (1, 0, 2))
    f = jnp.transpose(filters, (1, 2, 0, 3))
    vmem = pl.BlockSpec(memory_space=pltpu.VMEM)
    dma = pltpu.SemaphoreType.DMA

    def run(*refs):
        kernel(n_width, factor, *refs)

    conv, grad, filt = pl.pallas_call(
        run,
        out_shape=[
            jax.ShapeDtypeStruct((rows, cin_dev, cols), BF16),
            jax.ShapeDtypeStruct((rows, cin_dev, cols), BF16),
            jax.ShapeDtypeStruct((9, cin_dev, n_out), F32),
        ],
        in_specs=[vmem] * 3,
        out_specs=[vmem] * 3,
        scratch_shapes=[
            pltpu.VMEM((rows, n_out, cols), BF16),
            pltpu.VMEM((rows, n_out, cols), BF16),
            pltpu.VMEM((3, n_out, 128), BF16),
            pltpu.VMEM((16, 3, cin_dev, 128), BF16),
            pltpu.VMEM((2, rows, cin_dev, 128), BF16),
            pltpu.VMEM((192, cols), BF16),
            pltpu.VMEM((4, 9, cin_dev, 128), F32),
            pltpu.VMEM((n_width, 9, 8, 128), F32),
            pltpu.VMEM((2, 2, rows, cin_dev, 128), F32),
            pltpu.VMEM((2, 2, rows, cin_dev, 128), F32),
            pltpu.VMEM((2, rows, cin_dev, cols), F32),
            dma((2, N_MSG)),
            dma((2, N_MSG)),
            dma((16,)),
            dma((16,)),
            dma((2,)),
            dma((2,)),
            dma((n_width,)),
            dma((n_width,)),
            dma((n_width,)),
            dma((n_width,)),
            dma((2, 2)),
            dma((2, 2)),
        ],
        compiler_params=pltpu.CompilerParams(
            collective_id=0, has_side_effects=True, vmem_limit_bytes=40 * 1024 * 1024
        ),
        name="conv_all",
    )(x, g, f)
    conv = jnp.transpose(conv, (1, 0, 2))
    grad = jnp.transpose(grad, (1, 0, 2))
    filt = jnp.transpose(filt.reshape(3, 3, cin_dev, n_out), (2, 0, 1, 3))
    return conv, grad, filt


def solution(mesh):
    in_specs = (P("chan", None, "width"), P("chan", None, None, None), P("chan", None, "width"))
    out_specs = (P("chan", None, "width"), P("chan", None, "width"), P("chan", None, None, None))
    return jax.shard_map(body, mesh=mesh, in_specs=in_specs, out_specs=out_specs, check_vma=False)
```

time: 345 us -> 60.5 us (0.18)
  waiting for transfers between devices: 138 us -> 0 us
  blocking collectives: 88.1 us -> 0 us
  local copies, waits for them, and re-layouts: 73.8 us -> 3.34 us
  Pallas kernels: 0 us -> 55.9 us
  starting transfers between devices: 14.8 us -> 0 us
  between operations: 15.1 us -> 0.65 us
  matrix products: 10 us -> 0 us
  other arithmetic: 3.53 us -> 0 us
    psum x1 -> x0, waiting for transfers between devices: 137 us -> none  [body(): filter_total = lax.psum(filter_sum, 'width')]
    unnamed x1 -> x0, blocking collectives: 88.1 us -> none
    pallas_call x0 -> x1, Pallas kernels: none -> 55.9 us  [body(): pl.pallas_call(run, out_shape=[jax.ShapeDtypeStruct((rows, cin_dev, cols)...]
    slice x4 -> x0, local copies, waits for them, and re-layouts: 35.7 us -> none  [the longest x2 34 us: stack_taps(): padded[:, first_row:first_row + rows, first_col:first_col + cols]]
    unnamed x66 -> x5, local copies, waits for them, and re-layouts: 29.6 us -> 2.34 us
    ppermute x4 -> x0, starting transfers between devices: 14.7 us -> none  [the longest x2 8.44 us: padded_2(): before = lax.ppermute(last, axis, up)]
    dot_general x3 -> x0, matrix products: 10 us -> none  [the longest x1 7.55 us: body(): input_sum = jnp.dot(block, grad_stack, preferred_element_type=jnp.float32)]
    reshape x3 -> x0, local copies, waits for them, and re-layouts: 5.78 us -> none  [the longest x1 3.5 us: body(): summed.reshape(cout_dev * lax.axis_size('chan'), rows, cols)]
  transfers between devices with their start and end apart: 6 -> 0, of which waited for: 2 -> 0; matrix products, arithmetic and copies ran while one was open for 9% -> 0% of each run, Pallas kernels for 0% -> 0%
where the time goes in v1:
time: 60.5 us; the launch traced here: 59.9 us
  Pallas kernels  55.9 us (92%)
  local copies, waits for them, and re-layouts  3.34 us (6%)
  between operations  0.65 us (1%)
    pallas_call x1, Pallas kernels, body(): pl.pallas_call(run, out_shape=[jax.ShapeDtypeStruct((rows, cin_dev, cols)...  55.9 us
    unnamed x5, local copies, waits for them, and re-layouts  2.34 us

profile of v1, /device:TPU:4, one launch (start us, length us, event | category | flops | bytes accessed | tf_op | source)
XLA Modules:
  0.0 59.9 jit_solution(10638566076791831497)
XLA Ops:
  0.6 0.0 copy-start
  0.6 1.0 %copy_bitcast_fusion = (bf16[2,32,768]{2,1,0:T(8,128)(2,1)S(1)}, bf16[2,32,768]{2,1,0:T(8,128)(2,1)S(1)}) fusion(bf16[32,2,768]{2,1,0:T(2,128)(2,1)} %param.5, bf16[32,2,768]{2,1,0:T(2,128)(2,1)} %param.3), kind=kLoop, calls=%fused_computation | loop fusion | bytes 393216 | tf_op jit(solution)/shard_map/transpose | solution.py:449
  1.7 0.0 copy-done
  1.7 55.9 %conv_all.1 = (bf16[2,32,768]{2,1,0:T(8,128)(2,1)S(1)}, bf16[2,32,768]{2,1,0:T(8,128)(2,1)S(1)}, f32[9,32,512]{2,1,0:T(8,128)S(1)}) custom-call(bf16[2,32,768]{2,1,0:T(8,128)(2,1)S(1)} %get-tuple-element.13.refs_0_, bf16[2,32,768]{2,1,0:T(8,128)(2,1)S(1)} %get-tuple-element.12.refs_1_, bf16[3,3,32,512]{3,2,1,0:T(8,128)(2,1)S(1)} %bitcast.11), custom_call_target="tpu_custom_call" | custom-call | tf_op jit(solution)/shard_map/conv_all/pallas_call | solution.py:457
  57.6 0.7 %copy.8 = bf16[32,2,768]{2,1,0:T(2,128)(2,1)} copy(bf16[32,2,768]{2,0,1:T(8,128)(2,1)S(1)} %bitcast.13) | data formatting | bytes 196608
  58.3 0.7 %copy.9 = bf16[32,2,768]{2,1,0:T(2,128)(2,1)} copy(bf16[32,2,768]{2,0,1:T(8,128)(2,1)S(1)} %bitcast.12) | data formatting | bytes 196608
  59.0 0.8 %copy.13 = f32[32,3,3,512]{3,0,2,1:T(8,128)} copy(f32[32,3,3,512]{3,0,2,1:T(8,128)S(1)} %bitcast.10) | data formatting | bytes 1179648
Async XLA Ops:
  0.6 1.1 %copy-start = (bf16[32,3,3,512]{3,0,2,1:T(8,128)(2,1)S(1)}, bf16[32,3,3,512]{3,0,2,1:T(8,128)(2,1)}, u32[]{:S(2)}) copy-start(bf16[32,3,3,512]{3,0,2,1:T(8,128)(2,1)} %param.4) | copy-start | bytes 884740

commit v2 on v1

--- a/solution.py
+++ b/solution.py
@@ -11,79 +11,96 @@
 BF16 = jnp.bfloat16
 F32 = jnp.float32
 
-Y_UP, Y_DOWN, ACROSS, CORE = "up", "down", "across", "core"
+Y_ONE, Y_TWO, Y_THREE, ACROSS, CORE = (1, 0, 0), (2, 0, 0), (3, 0, 0), (0, 1, 0), (0, 0, 1)
+ALONG = [Y_ONE, Y_THREE, Y_TWO]
 
 
 def arrived(piece, way):
     h, dy, dx, dc = piece
-    if way == Y_UP:
-        return (h, (dy - 1) % 4, dx, dc)
-    if way == Y_DOWN:
-        return (h, (dy + 1) % 4, dx, dc)
-    if way == ACROSS:
-        return (h, dy, 1 - dx, dc)
-    return (h, dy, dx, 1 - dc)
-
-
-def gather_plan(relay):
-    first = [
-        ((0, 0, 0, 0), Y_UP),
-        ((0, 0, 0, 0), Y_DOWN),
-        ((1, 0, 0, 0), ACROSS),
-        ((1, 0, 0, 0), Y_UP),
-        ((1, 0, 0, 0), Y_DOWN),
-        ((0, 0, 0, 0), ACROSS),
-        ((0, 0, 0, 0), CORE),
-        ((1, 0, 0, 0), CORE),
-    ]
-    up = [Y_UP] if relay == Y_UP else []
-    down = [Y_DOWN] if relay == Y_DOWN else []
-    stages = [
-        [(None, first)],
-        [
-            ((1, 0, 1, 0), [Y_UP, Y_DOWN, CORE]),
-            ((0, 3, 0, 0), up + [ACROSS, CORE]),
-            ((0, 1, 0, 0), down + [ACROSS, CORE]),
-            ((1, 3, 0, 0), [Y_UP, CORE]),
-            ((1, 1, 0, 0), [CORE]),
-            ((0, 0, 1, 0), [CORE]),
-        ],
-        [
-            ((1, 1, 1, 0), [Y_DOWN, CORE]),
-            ((1, 3, 1, 0), [CORE]),
-            ((0, 2, 0, 0), [ACROSS, CORE]),
-            ((0, 3, 1, 0), [CORE]),
-            ((0, 1, 1, 0), [CORE]),
-            ((1, 2, 0, 0), [CORE]),
-        ],
-        [
-            ((1, 2, 1, 0), [CORE]),
-            ((0, 2, 1, 0), [CORE]),
-        ],
-    ]
-    plan = []
-    for stage in stages:
-        steps = []
-        for piece, sends in stage:
-            if piece is not None:
-                sends = [(piece, way) for way in sends]
-            steps.append((piece, sends))
-        plan.append(steps)
-    return plan
-
-
-def message_ids(plan):
-    brings, number = {}, {}
-    for steps in plan:
-        for _, sends in steps:
-            for piece, way in sends:
+    return (h, (dy - way[0]) % 4, (dx + way[1]) % 2, (dc + way[2]) % 2)
+
+
+OWN = (0, 0, 0)
+STAGES = [
+    [
+        ((1,) + OWN, [ACROSS]),
+        ((0,) + OWN, [ACROSS] + ALONG),
+        ((1,) + OWN, ALONG),
+        ((0,) + OWN, [CORE]),
+        ((1,) + OWN, [CORE]),
+    ],
+    [
+        ((1, 0, 1, 0), ALONG + [CORE]),
+        ((0, 0, 1, 0), [CORE]),
+    ],
+    [
+        ((0, 1, 0, 0), [ACROSS, CORE]),
+        ((0, 3, 0, 0), [ACROSS, CORE]),
+        ((0, 2, 0, 0), [ACROSS, CORE]),
+        ((1, 1, 0, 0), [CORE]),
+        ((1, 3, 0, 0), [CORE]),
+        ((1, 2, 0, 0), [CORE]),
+    ],
+    [
+        ((1, 1, 1, 0), [CORE]),
+        ((1, 3, 1, 0), [CORE]),
+        ((0, 1, 1, 0), [CORE]),
+        ((0, 3, 1, 0), [CORE]),
+    ],
+    [
+        ((1, 2, 1, 0), [CORE]),
+        ((0, 2, 1, 0), [CORE]),
+    ],
+]
+
+STAGES_X = [
+    [
+        ((1,) + OWN, [ACROSS]),
+        ((0,) + OWN, [ACROSS]),
+        ((1,) + OWN, ALONG),
+        ((0,) + OWN, ALONG),
+        ((0,) + OWN, [CORE]),
+        ((1,) + OWN, [CORE]),
+    ],
+    [
+        ((1, 0, 1, 0), ALONG + [CORE]),
+        ((0, 0, 1, 0), ALONG + [CORE]),
+    ],
+    [
+        ((1, 1, 0, 0), [CORE]),
+        ((1, 3, 0, 0), [CORE]),
+        ((0, 1, 0, 0), [CORE]),
+        ((0, 3, 0, 0), [CORE]),
+        ((1, 2, 0, 0), [CORE]),
+        ((0, 2, 0, 0), [CORE]),
+    ],
+    [
+        ((1, 1, 1, 0), [CORE]),
+        ((1, 3, 1, 0), [CORE]),
+        ((0, 1, 1, 0), [CORE]),
+        ((0, 3, 1, 0), [CORE]),
+    ],
+    [
+        ((1, 2, 1, 0), [CORE]),
+        ((0, 2, 1, 0), [CORE]),
+    ],
+]
+
+
+def message_ids(stages):
+    number, brings = {}, {}
+    for steps in stages:
+        for piece, ways in steps:
+            for way in ways:
                 number[(piece, way)] = len(number)
                 brings[arrived(piece, way)] = number[(piece, way)]
-    return brings, number
-
-
-PLANS = [gather_plan(Y_UP), gather_plan(Y_DOWN)]
-N_MSG = 30
+    return number, brings
+
+
+PLANS = [STAGES, STAGES_X]
+IDS = [message_ids(stages) for stages in PLANS]
+N_MSG = 32
+Z_ORDER = [1, 7, 2, 6, 3, 5, 4]
 
 
 def kernel(
@@ -102,7 +119,10 @@
     halo,
     xs,
     part,
+    pair_out,
+    pair_in,
     rs_buf,
+    blocks,
     e_out,
     e_in,
     y_buf,
@@ -112,6 +132,8 @@
     f_recv,
     halo_send,
     halo_recv,
+    pair_send,
+    pair_recv,
     rs_send,
     rs_recv,
     ag_send,
@@ -125,6 +147,10 @@
     px = (k // 2) % 2
     pc = k % 2
     cols = x_ref.shape[2]
+    n_z = n_width // 2
+    z = w // 2
+    column = w % 2
+    across = w + 1 - 2 * column
     right = lax.rem(w + 1, n_width)
     left = lax.rem(w + n_width - 1, n_width)
 
@@ -134,22 +160,14 @@
         c = 1 - pc if dc else pc
         return y * 4 + x * 2 + c
 
-    ways = {
-        Y_UP: chan_of(1, 0, 0),
-        Y_DOWN: chan_of(3, 0, 0),
-        ACROSS: chan_of(0, 1, 0),
-        CORE: chan_of(0, 0, 1),
-    }
-
     barrier = pltpu.get_barrier_semaphore()
     for d in range(1, 16):
         pl.semaphore_signal(
             barrier, inc=1, device_id={"chan": lax.rem(k + d, 16)}, device_id_type=MESH
         )
-    for d in range(1, n_width):
-        pl.semaphore_signal(
-            barrier, inc=1, device_id={"width": lax.rem(w + d, n_width)}, device_id_type=MESH
-        )
+    near_width = [lax.rem(w + 2 * d, n_width) for d in range(1, n_z)] + [right, left]
+    for device in near_width:
+        pl.semaphore_signal(barrier, inc=1, device_id={"width": device}, device_id_type=MESH)
 
     lane = lax.broadcasted_iota(jnp.int32, (96, 128), 1)
 
@@ -174,7 +192,7 @@
     g_all[:, own_rows(k), :] = g_ref[...]
     f_all[:, own_rows(k), :] = f_msg[k]
 
-    pl.semaphore_wait(barrier, 15 + n_width - 1)
+    pl.semaphore_wait(barrier, 15 + len(near_width))
 
     pending = []
 
@@ -183,46 +201,44 @@
         pending.append(copy)
 
     arrays = [(g_all, g_ref), (x_all, x_ref)]
-    brings_of = [message_ids(plan)[0] for plan in PLANS]
-    number_of = [message_ids(plan)[1] for plan in PLANS]
 
     def piece_ref(which, piece):
         h, dy, dx, dc = piece
         return arrays[which][0].at[h, own_rows(chan_of(dy, dx, dc)), :]
 
     def gather_send(which, piece, way):
-        m = number_of[which][(piece, way)]
+        m = IDS[which][0][(piece, way)]
         ref = piece_ref(which, piece)
-        src = arrays[which][1].at[piece[0]] if piece[1:] == (0, 0, 0) else ref
+        src = arrays[which][1].at[piece[0]] if piece[1:] == OWN else ref
         start(
             pltpu.make_async_remote_copy(
                 src_ref=src,
                 dst_ref=ref,
                 send_sem=gat_send.at[which, m],
                 recv_sem=gat_recv.at[which, m],
-                device_id={"chan": ways[way]},
+                device_id={"chan": chan_of(*way)},
                 device_id_type=MESH,
             )
         )
 
     def gather_wait(which, piece):
-        m = brings_of[which][piece]
+        m = IDS[which][1][piece]
         ref = piece_ref(which, piece)
         pltpu.make_async_remote_copy(
             src_ref=ref,
             dst_ref=ref,
             send_sem=gat_send.at[which, m],
             recv_sem=gat_recv.at[which, m],
-            device_id={"chan": ways[CORE]},
+            device_id={"chan": chan_of(*CORE)},
             device_id_type=MESH,
         ).wait_recv()
 
     def gather_stage(which, number):
-        for piece, sends in PLANS[which][number]:
-            if piece is not None:
+        for piece, ways in PLANS[which][number]:
+            if piece[1:] != OWN:
                 gather_wait(which, piece)
-            for sent, way in sends:
-                gather_send(which, sent, way)
+            for way in ways:
+                gather_send(which, piece, way)
 
     def gather_class(which, dy):
         for dx in range(2):
@@ -263,18 +279,42 @@
         lane64 == 127, from_right, xs[128:192, cols - 128 : cols].astype(F32)
     ).astype(BF16)
 
-    def rs_copy(block, slot, device):
+    def group_of(dy):
+        return lax.rem(py + dy, 4)
+
+    def rs_copy(dy, d):
         return pltpu.make_async_remote_copy(
-            src_ref=part.at[block % 4, :, pl.ds(pl.multiple_of(block // 4 * 8, 8), 8), :],
-            dst_ref=rs_buf.at[slot],
-            send_sem=rs_send.at[block],
-            recv_sem=rs_recv.at[slot],
+            src_ref=part.at[group_of(dy), pl.ds(2 * lax.rem(z + d, n_z), 2)],
+            dst_ref=rs_buf.at[d, group_of(dy)],
+            send_sem=rs_send.at[dy, d],
+            recv_sem=rs_recv.at[dy, d],
+            device_id={"width": lax.rem(w + 2 * d, n_width)},
+            device_id_type=MESH,
+        )
+
+    def pair_copy(dy):
+        return pltpu.make_async_remote_copy(
+            src_ref=pair_out.at[dy],
+            dst_ref=pair_in.at[dy],
+            send_sem=pair_send.at[dy],
+            recv_sem=pair_recv.at[dy],
+            device_id={"width": across},
+            device_id_type=MESH,
+        )
+
+    def ag_copy(dy, index, slot, device):
+        ref = blocks.at[group_of(dy), index]
+        return pltpu.make_async_remote_copy(
+            src_ref=ref,
+            dst_ref=ref,
+            send_sem=ag_send.at[dy, slot],
+            recv_sem=ag_recv.at[dy, slot],
             device_id={"width": device},
             device_id_type=MESH,
         )
 
     def filter_class(dy):
-        group = lax.rem(py + dy, 4)
+        group = group_of(dy)
         rows = pl.ds(pl.multiple_of(group * 128, 128), 128)
         taps = [
             lax.dot_general(
@@ -284,19 +324,37 @@
         ]
         for b in range(3):
             one, two = slice(b * 64, b * 64 + 32), slice(b * 64 + 32, b * 64 + 64)
-            part[group, b] = taps[1][one]
-            part[group, 3 + b] = taps[0][one] + taps[1][two]
-            part[group, 6 + b] = taps[0][two]
-        for c8 in range(4):
-            block = c8 * 4 + group
-
-            @pl.when(block != w)
-            def _():
-                rs_copy(block, w, block).start()
-
-            @pl.when(block == w)
-            def _():
-                rs_buf[w] = part[group, :, c8 * 8 : c8 * 8 + 8, :]
+            three = [taps[1][one], taps[0][one] + taps[1][two], taps[0][two]]
+            for a in range(3):
+                part[group, :, a * 3 + b] = three[a].reshape(n_width, 2, 128)
+        for d in Z_ORDER:
+            start(rs_copy(dy, d))
+
+    def sum_along_z(dy):
+        group = group_of(dy)
+        for d in Z_ORDER:
+            rs_copy(dy, d).wait_recv()
+        for side in range(2):
+            total = part[group, 2 * z + side]
+            for d in range(1, n_z):
+                total = total + rs_buf[d, group, side]
+            part[group, 2 * z + side] = total
+        pair_out[dy] = part[group, across]
+        start(pair_copy(dy))
+
+    def hand_out(dy):
+        group = group_of(dy)
+        pair_copy(dy).wait_recv()
+        blocks[group, w] = (part[group, w] + pair_in[dy]) * factor
+        for d in Z_ORDER:
+            start(ag_copy(dy, w, d, lax.rem(w + 2 * d, n_width)))
+        start(ag_copy(dy, w, n_z, across))
+
+    def relay(dy):
+        for d in Z_ORDER:
+            source = lax.rem(w + n_width - 2 * d, n_width)
+            ag_copy(dy, source, d, across).wait_recv()
+            start(ag_copy(dy, source, n_z + d, across))
 
     def f_copy(d):
         return pltpu.make_async_remote_copy(
@@ -310,18 +368,24 @@
 
     gather_class(0, 0)
     filter_class(0)
-    gather_stage(1, 0)
     gather_stage(0, 2)
+    gather_stage(0, 3)
+    gather_class(0, 1)
+    filter_class(1)
     gather_class(0, 3)
     filter_class(3)
-    gather_class(0, 1)
-    filter_class(1)
-    gather_stage(0, 3)
+    gather_stage(0, 4)
+    gather_class(0, 2)
+    filter_class(2)
+    gather_stage(1, 0)
+    sum_along_z(0)
     gather_stage(1, 1)
     for d in range(1, 16):
         start(f_copy(d))
-    gather_class(0, 2)
-    filter_class(2)
+    sum_along_z(1)
+    hand_out(0)
+    sum_along_z(3)
+    hand_out(1)
     gather_stage(1, 2)
 
     lane32 = lax.broadcasted_iota(jnp.int32, (32, cols), 1)
@@ -370,40 +434,14 @@
     taps = [[sums[h * 96 + b * 32 : h * 96 + b * 32 + 32] for b in (2, 1, 0)] for h in range(2)]
     grad_copies = edges_out(1, taps)
 
+    sum_along_z(2)
+    hand_out(3)
     gather_stage(1, 3)
-
-    for d in range(1, n_width):
-        source = lax.rem(w + d, n_width)
-        rs_copy(source, source, source).wait_recv()
-    total = rs_buf[0]
-    for s in range(1, n_width):
-        total = total + rs_buf[s]
-
-    def block_ref(index):
-        return filt_ref.at[
-            :,
-            pl.ds(pl.multiple_of(index // 4 * 8, 8), 8),
-            pl.ds(pl.multiple_of(index % 4 * 128, 128), 128),
-        ]
-
-    filt_ref[
-        :,
-        pl.ds(pl.multiple_of(w // 4 * 8, 8), 8),
-        pl.ds(pl.multiple_of(w % 4 * 128, 128), 128),
-    ] = total * factor
-
-    def ag_copy(index, d, device):
-        return pltpu.make_async_remote_copy(
-            src_ref=block_ref(index),
-            dst_ref=block_ref(index),
-            send_sem=ag_send.at[d],
-            recv_sem=ag_recv.at[d],
-            device_id={"width": device},
-            device_id_type=MESH,
-        )
-
-    for d in range(1, n_width):
-        start(ag_copy(w, d, lax.rem(w + d, n_width)))
+    gather_stage(1, 4)
+    hand_out(2)
+    relay(0)
+    relay(1)
+    relay(3)
 
     for which_dy in range(4):
         gather_class(1, which_dy)
@@ -427,17 +465,21 @@
         )
         taps.append([sums[b * 32 : b * 32 + 32] for b in range(3)])
     conv_copies = edges_out(0, taps)
+    relay(2)
     edges_in(1, grad_copies, grad_ref)
     edges_in(0, conv_copies, conv_ref)
 
-    for d in range(1, n_width):
-        source = lax.rem(w + n_width - d, n_width)
-        ag_copy(source, d, source).wait_recv()
+    for dy in (0, 1, 3, 2):
+        for d in range(n_z):
+            source = lax.rem(across + n_width - 2 * d, n_width)
+            ag_copy(dy, source, n_z + d, across).wait_recv()
+    for group in range(4):
+        for tap in range(9):
+            filt_ref[tap, :, group * 128 : group * 128 + 128] = blocks[group, :, tap].reshape(
+                2 * n_width, 128
+            )
     for copy in pending:
         copy.wait_send()
-    for d in range(1, n_width):
-        block = lax.rem(w + d, n_width)
-        rs_copy(block, w, block).wait_send()
 
 
 def body(activations, filters, cotangent):
@@ -470,8 +512,11 @@
             pltpu.VMEM((16, 3, cin_dev, 128), BF16),
             pltpu.VMEM((2, rows, cin_dev, 128), BF16),
             pltpu.VMEM((192, cols), BF16),
-            pltpu.VMEM((4, 9, cin_dev, 128), F32),
-            pltpu.VMEM((n_width, 9, 8, 128), F32),
+            pltpu.VMEM((4, n_width, 9, 2, 128), F32),
+            pltpu.VMEM((4, 9, 2, 128), F32),
+            pltpu.VMEM((4, 9, 2, 128), F32),
+            pltpu.VMEM((n_width // 2, 4, 2, 9, 2, 128), F32),
+            pltpu.VMEM((4, n_width, 9, 2, 128), F32),
             pltpu.VMEM((2, 2, rows, cin_dev, 128), F32),
             pltpu.VMEM((2, 2, rows, cin_dev, 128), F32),
             pltpu.VMEM((2, rows, cin_dev, cols), F32),
@@ -481,10 +526,12 @@
             dma((16,)),
             dma((2,)),
             dma((2,)),
-            dma((n_width,)),
-            dma((n_width,)),
-            dma((n_width,)),
-            dma((n_width,)),
+            dma((4,)),
+            dma((4,)),
+            dma((4, n_width // 2)),
+            dma((4, n_width // 2)),
+            dma((4, n_width)),
+            dma((4, n_width)),
             dma((2, 2)),
             dma((2, 2)),
         ],

time: 60.5 us -> 54.9 us (0.907)
  the two profiles are of different devices: /device:TPU:4 before, /device:TPU:8 now
where the time goes in v2:
time: 54.9 us; the launch traced here: 54.8 us
  Pallas kernels  50.8 us (93%)
  local copies, waits for them, and re-layouts  3.34 us (6%)
  between operations  0.65 us (1%)
    pallas_call x1, Pallas kernels, body(): pl.pallas_call(run, out_shape=[jax.ShapeDtypeStruct((rows, cin_dev, cols)...  50.8 us
    unnamed x5, local copies, waits for them, and re-layouts  2.34 us

profile of v2, /device:TPU:8, one launch (start us, length us, event | category | flops | bytes accessed | tf_op | source)
XLA Modules:
  0.0 54.8 jit_solution(9199773953726722999)
XLA Ops:
  0.6 0.0 copy-start
  0.6 1.0 %copy_bitcast_fusion = (bf16[2,32,768]{2,1,0:T(8,128)(2,1)S(1)}, bf16[2,32,768]{2,1,0:T(8,128)(2,1)S(1)}) fusion(bf16[32,2,768]{2,1,0:T(2,128)(2,1)} %param.5, bf16[32,2,768]{2,1,0:T(2,128)(2,1)} %param.3), kind=kLoop, calls=%fused_computation | loop fusion | bytes 393216 | tf_op jit(solution)/shard_map/transpose | solution.py:491
  1.7 0.0 copy-done
  1.7 50.8 %conv_all.1 = (bf16[2,32,768]{2,1,0:T(8,128)(2,1)S(1)}, bf16[2,32,768]{2,1,0:T(8,128)(2,1)S(1)}, f32[9,32,512]{2,1,0:T(8,128)S(1)}) custom-call(bf16[2,32,768]{2,1,0:T(8,128)(2,1)S(1)} %get-tuple-element.13.refs_0_, bf16[2,32,768]{2,1,0:T(8,128)(2,1)S(1)} %get-tuple-element.12.refs_1_, bf16[3,3,32,512]{3,2,1,0:T(8,128)(2,1)S(1)} %bitcast.11), custom_call_target="tpu_custom_call" | custom-call | tf_op jit(solution)/shard_map/conv_all/pallas_call | solution.py:499
  52.5 0.7 %copy.8 = bf16[32,2,768]{2,1,0:T(2,128)(2,1)} copy(bf16[32,2,768]{2,0,1:T(8,128)(2,1)S(1)} %bitcast.13) | data formatting | bytes 196608
  53.2 0.7 %copy.9 = bf16[32,2,768]{2,1,0:T(2,128)(2,1)} copy(bf16[32,2,768]{2,0,1:T(8,128)(2,1)S(1)} %bitcast.12) | data formatting | bytes 196608
  53.9 0.8 %copy.13 = f32[32,3,3,512]{3,0,2,1:T(8,128)} copy(f32[32,3,3,512]{3,0,2,1:T(8,128)S(1)} %bitcast.10) | data formatting | bytes 1179648
Async XLA Ops:
  0.6 1.1 %copy-start = (bf16[32,3,3,512]{3,0,2,1:T(8,128)(2,1)S(1)}, bf16[32,3,3,512]{3,0,2,1:T(8,128)(2,1)}, u32[]{:S(2)}) copy-start(bf16[32,3,3,512]{3,0,2,1:T(8,128)(2,1)} %param.4) | copy-start | bytes 884740

commit v3 on v2

--- a/solution.py
+++ b/solution.py
@@ -101,6 +101,7 @@
 IDS = [message_ids(stages) for stages in PLANS]
 N_MSG = 32
 Z_ORDER = [1, 7, 2, 6, 3, 5, 4]
+BOTH = (2,)
 
 
 def kernel(
@@ -111,7 +112,7 @@
     f_ref,
     conv_ref,
     grad_ref,
-    filt_ref,
+    blocks,
     x_all,
     g_all,
     f_all,
@@ -119,10 +120,8 @@
     halo,
     xs,
     part,
-    pair_out,
     pair_in,
     rs_buf,
-    blocks,
     e_out,
     e_in,
     y_buf,
@@ -169,28 +168,8 @@
     for device in near_width:
         pl.semaphore_signal(barrier, inc=1, device_id={"width": device}, device_id_type=MESH)
 
-    lane = lax.broadcasted_iota(jnp.int32, (96, 128), 1)
-
-    for tile in range(4):
-        parts = [
-            f_ref[:, b, :, tile * 128 : tile * 128 + 128].reshape(96, 128).astype(F32)
-            for b in range(3)
-        ]
-        for j in range(4):
-            out = jnp.zeros((96, 128), F32)
-            for b in range(3):
-                moved = parts[b]
-                if (b - j) % 4:
-                    moved = pltpu.roll(moved, ((b - j) % 4) * 32, 1)
-                out = jnp.where(lane // 32 == b, moved, out)
-            f_msg[tile * 4 + j] = out.astype(BF16).reshape(3, 32, 128)
-
     def own_rows(index):
         return pl.ds(pl.multiple_of(index * 32, 32), 32)
-
-    x_all[:, own_rows(k), :] = x_ref[...]
-    g_all[:, own_rows(k), :] = g_ref[...]
-    f_all[:, own_rows(k), :] = f_msg[k]
 
     pl.semaphore_wait(barrier, 15 + len(near_width))
 
@@ -257,9 +236,12 @@
         )
 
     halo_copies = [halo_copy(0, right), halo_copy(1, left)]
+    gather_stage(0, 0)
     for copy in halo_copies:
         start(copy)
-    gather_stage(0, 0)
+
+    x_all[:, own_rows(k), :] = x_ref[...]
+    g_all[:, own_rows(k), :] = g_ref[...]
 
     lane64 = lax.broadcasted_iota(jnp.int32, (64, 128), 1)
     mine = x_ref[...].reshape(64, cols)
@@ -294,8 +276,8 @@
 
     def pair_copy(dy):
         return pltpu.make_async_remote_copy(
-            src_ref=pair_out.at[dy],
-            dst_ref=pair_in.at[dy],
+            src_ref=part.at[group_of(dy), pl.ds(2 * z, 2) if dy in BOTH else pl.ds(across, 1)],
+            dst_ref=pair_in.at[dy, pl.ds(0, 2 if dy in BOTH else 1)],
             send_sem=pair_send.at[dy],
             recv_sem=pair_recv.at[dy],
             device_id={"width": across},
@@ -303,7 +285,8 @@
         )
 
     def ag_copy(dy, index, slot, device):
-        ref = blocks.at[group_of(dy), index]
+        owners = pl.ds(2 * (index // 2), 2) if dy in BOTH else pl.ds(index, 1)
+        ref = blocks.at[group_of(dy), owners]
         return pltpu.make_async_remote_copy(
             src_ref=ref,
             dst_ref=ref,
@@ -339,22 +322,28 @@
             for d in range(1, n_z):
                 total = total + rs_buf[d, group, side]
             part[group, 2 * z + side] = total
-        pair_out[dy] = part[group, across]
         start(pair_copy(dy))
 
     def hand_out(dy):
         group = group_of(dy)
         pair_copy(dy).wait_recv()
-        blocks[group, w] = (part[group, w] + pair_in[dy]) * factor
+        if dy in BOTH:
+            for side in range(2):
+                total = part[group, 2 * z + side] + pair_in[dy, side]
+                blocks[group, 2 * z + side] = total * factor
+        else:
+            blocks[group, w] = (part[group, w] + pair_in[dy, 0]) * factor
         for d in Z_ORDER:
             start(ag_copy(dy, w, d, lax.rem(w + 2 * d, n_width)))
-        start(ag_copy(dy, w, n_z, across))
+        if dy not in BOTH:
+            start(ag_copy(dy, w, n_z, across))
 
     def relay(dy):
         for d in Z_ORDER:
             source = lax.rem(w + n_width - 2 * d, n_width)
             ag_copy(dy, source, d, across).wait_recv()
-            start(ag_copy(dy, source, n_z + d, across))
+            if dy not in BOTH:
+                start(ag_copy(dy, source, n_z + d, across))
 
     def f_copy(d):
         return pltpu.make_async_remote_copy(
@@ -368,6 +357,24 @@
 
     gather_class(0, 0)
     filter_class(0)
+    lane = lax.broadcasted_iota(jnp.int32, (96, 128), 1)
+
+    for tile in range(4):
+        parts = [
+            f_ref[:, b, :, tile * 128 : tile * 128 + 128].reshape(96, 128).astype(F32)
+            for b in range(3)
+        ]
+        for j in range(4):
+            out = jnp.zeros((96, 128), F32)
+            for b in range(3):
+                moved = parts[b]
+                if (b - j) % 4:
+                    moved = pltpu.roll(moved, ((b - j) % 4) * 32, 1)
+                out = jnp.where(lane // 32 == b, moved, out)
+            f_msg[tile * 4 + j] = out.astype(BF16).reshape(3, 32, 128)
+
+    f_all[:, own_rows(k), :] = f_msg[k]
+
     gather_stage(0, 2)
     gather_stage(0, 3)
     gather_class(0, 1)
@@ -470,16 +477,22 @@
     edges_in(0, conv_copies, conv_ref)
 
     for dy in (0, 1, 3, 2):
-        for d in range(n_z):
+        for d in range(0 if dy in BOTH else n_z):
             source = lax.rem(across + n_width - 2 * d, n_width)
             ag_copy(dy, source, n_z + d, across).wait_recv()
-    for group in range(4):
+    for copy in pending:
+        copy.wait_send()
+
+
+def finish(conv_in, grad_in, blocks, conv_ref, grad_ref, filt_ref):
+    for group in range(blocks.shape[0]):
         for tap in range(9):
             filt_ref[tap, :, group * 128 : group * 128 + 128] = blocks[group, :, tap].reshape(
-                2 * n_width, 128
+                filt_ref.shape[1], 128
             )
-    for copy in pending:
-        copy.wait_send()
+    for source, target in ((conv_in, conv_ref), (grad_in, grad_ref)):
+        for h in range(2):
+            target[:, h, :] = source[h]
 
 
 def body(activations, filters, cotangent):
@@ -501,7 +514,7 @@
         out_shape=[
             jax.ShapeDtypeStruct((rows, cin_dev, cols), BF16),
             jax.ShapeDtypeStruct((rows, cin_dev, cols), BF16),
-            jax.ShapeDtypeStruct((9, cin_dev, n_out), F32),
+            jax.ShapeDtypeStruct((4, n_width, 9, 2, 128), F32),
         ],
         in_specs=[vmem] * 3,
         out_specs=[vmem] * 3,
@@ -513,10 +526,8 @@
             pltpu.VMEM((2, rows, cin_dev, 128), BF16),
             pltpu.VMEM((192, cols), BF16),
             pltpu.VMEM((4, n_width, 9, 2, 128), F32),
-            pltpu.VMEM((4, 9, 2, 128), F32),
-            pltpu.VMEM((4, 9, 2, 128), F32),
+            pltpu.VMEM((4, 2, 9, 2, 128), F32),
             pltpu.VMEM((n_width // 2, 4, 2, 9, 2, 128), F32),
-            pltpu.VMEM((4, n_width, 9, 2, 128), F32),
             pltpu.VMEM((2, 2, rows, cin_dev, 128), F32),
             pltpu.VMEM((2, 2, rows, cin_dev, 128), F32),
             pltpu.VMEM((2, rows, cin_dev, cols), F32),
@@ -536,12 +547,22 @@
             dma((2, 2)),
         ],
         compiler_params=pltpu.CompilerParams(
-            collective_id=0, has_side_effects=True, vmem_limit_bytes=40 * 1024 * 1024
+            collective_id=0, has_side_effects=True, vmem_limit_bytes=20 * 1024 * 1024
         ),
         name="conv_all",
     )(x, g, f)
-    conv = jnp.transpose(conv, (1, 0, 2))
-    grad = jnp.transpose(grad, (1, 0, 2))
+    conv, grad, filt = pl.pallas_call(
+        finish,
+        out_shape=[
+            jax.ShapeDtypeStruct((cin_dev, rows, cols), BF16),
+            jax.ShapeDtypeStruct((cin_dev, rows, cols), BF16),
+            jax.ShapeDtypeStruct((9, cin_dev, n_out), F32),
+        ],
+        in_specs=[vmem] * 3,
+        out_specs=[vmem] * 3,
+        compiler_params=pltpu.CompilerParams(vmem_limit_bytes=8 * 1024 * 1024),
+        name="finish",
+    )(conv, grad, filt)
     filt = jnp.transpose(filt.reshape(3, 3, cin_dev, n_out), (2, 0, 1, 3))
     return conv, grad, filt
 

time: 54.9 us -> 52.5 us (0.956)
  the two profiles are of different devices: /device:TPU:8 before, /device:TPU:4 now
where the time goes in v3:
time: 52.5 us; the launch traced here: 52.4 us
  Pallas kernels  50.7 us (97%)
  local copies, waits for them, and re-layouts  1.05 us (2%)
  between operations  0.65 us (1%)
    pallas_call x1, Pallas kernels, body(): pl.pallas_call(run, out_shape=[jax.ShapeDtypeStruct((rows, cin_dev, cols)...  49.7 us

profile of v3, /device:TPU:4, one launch (start us, length us, event | category | flops | bytes accessed | tf_op | source)
XLA Modules:
  0.0 52.4 jit_solution(10272726454702271511)
XLA Ops:
  0.6 0.0 copy-start
  0.6 1.0 %copy_bitcast_fusion = (bf16[2,32,768]{2,1,0:T(8,128)(2,1)S(1)}, bf16[2,32,768]{2,1,0:T(8,128)(2,1)S(1)}) fusion(bf16[32,2,768]{2,1,0:T(2,128)(2,1)} %param.5, bf16[32,2,768]{2,1,0:T(2,128)(2,1)} %param.3), kind=kLoop, calls=%fused_computation | loop fusion | bytes 393216 | tf_op jit(solution)/shard_map/transpose | solution.py:504
  1.6 0.0 copy-done
  1.7 49.7 %conv_all.1 = (bf16[2,32,768]{2,1,0:T(8,128)(2,1)S(1)}, bf16[2,32,768]{2,1,0:T(8,128)(2,1)S(1)}, f32[4,16,9,2,128]{4,3,2,1,0:T(2,128)S(1)}) custom-call(bf16[2,32,768]{2,1,0:T(8,128)(2,1)S(1)} %get-tuple-element.16.refs_0_, bf16[2,32,768]{2,1,0:T(8,128)(2,1)S(1)} %get-tuple-element.15.refs_1_, bf16[3,3,32,512]{3,2,1,0:T(8,128)(2,1)S(1)} %bitcast.8), custom_call_target="tpu_custom_call" | custom-call | tf_op jit(solution)/shard_map/conv_all/pallas_call | solution.py:512
  51.4 1.0 %finish.1 = (bf16[32,2,768]{2,1,0:T(2,128)(2,1)}, bf16[32,2,768]{2,1,0:T(2,128)(2,1)}, f32[9,32,512]{2,1,0:T(8,128)}) custom-call(bf16[2,32,768]{2,1,0:T(8,128)(2,1)S(1)} %get-tuple-element.9.conv_in, bf16[2,32,768]{2,1,0:T(8,128)(2,1)S(1)} %get-tuple-element.10.grad_in, f32[4,16,9,2,128]{4,3,2,1,0:T(2,128)S(1)} %get-tuple-element.11.blocks), custom_call_target="tpu_custom_call" | custom-call | tf_op jit(solution)/shard_map/finish/pallas_call | solution.py:554
Async XLA Ops:
  0.6 1.1 %copy-start = (bf16[32,3,3,512]{3,0,2,1:T(8,128)(2,1)S(1)}, bf16[32,3,3,512]{3,0,2,1:T(8,128)(2,1)}, u32[]{:S(2)}) copy-start(bf16[32,3,3,512]{3,0,2,1:T(8,128)(2,1)} %param.4) | copy-start | bytes 884740

commit v4 on v3

--- a/solution.py
+++ b/solution.py
@@ -12,7 +12,7 @@
 F32 = jnp.float32
 
 Y_ONE, Y_TWO, Y_THREE, ACROSS, CORE = (1, 0, 0), (2, 0, 0), (3, 0, 0), (0, 1, 0), (0, 0, 1)
-ALONG = [Y_ONE, Y_THREE, Y_TWO]
+ALONG = [Y_TWO, Y_ONE, Y_THREE]
 
 
 def arrived(piece, way):
@@ -100,7 +100,7 @@
 PLANS = [STAGES, STAGES_X]
 IDS = [message_ids(stages) for stages in PLANS]
 N_MSG = 32
-Z_ORDER = [1, 7, 2, 6, 3, 5, 4]
+Z_ORDER = [4, 3, 5, 2, 6, 1, 7]
 BOTH = (2,)
 
 
@@ -392,7 +392,6 @@
     sum_along_z(1)
     hand_out(0)
     sum_along_z(3)
-    hand_out(1)
     gather_stage(1, 2)
 
     lane32 = lax.broadcasted_iota(jnp.int32, (32, cols), 1)
@@ -442,6 +441,7 @@
     grad_copies = edges_out(1, taps)
 
     sum_along_z(2)
+    hand_out(1)
     hand_out(3)
     gather_stage(1, 3)
     gather_stage(1, 4)

time: 52.5 us -> 51.9 us (0.989)
  Pallas kernels: 50.7 us -> 50.1 us
    pallas_call x1, Pallas kernels: 49.7 us -> 49.1 us  [body(): pl.pallas_call(run, out_shape=[jax.ShapeDtypeStruct((rows, cin_dev, cols)...]
where the time goes in v4:
time: 51.9 us; the launch traced here: 51.8 us
  Pallas kernels  50.1 us (97%)
  local copies, waits for them, and re-layouts  1.05 us (2%)
  between operations  0.65 us (1%)
    pallas_call x1, Pallas kernels, body(): pl.pallas_call(run, out_shape=[jax.ShapeDtypeStruct((rows, cin_dev, cols)...  49.1 us

profile of v4, /device:TPU:4, one launch (start us, length us, event | category | flops | bytes accessed | tf_op | source)
XLA Modules:
  0.0 51.8 jit_solution(6841967521509991290)
XLA Ops:
  0.6 0.0 copy-start
  0.6 1.0 %copy_bitcast_fusion = (bf16[2,32,768]{2,1,0:T(8,128)(2,1)S(1)}, bf16[2,32,768]{2,1,0:T(8,128)(2,1)S(1)}) fusion(bf16[32,2,768]{2,1,0:T(2,128)(2,1)} %param.5, bf16[32,2,768]{2,1,0:T(2,128)(2,1)} %param.3), kind=kLoop, calls=%fused_computation | loop fusion | bytes 393216 | tf_op jit(solution)/shard_map/transpose | solution.py:504
  1.6 0.0 copy-done
  1.7 49.1 %conv_all.1 = (bf16[2,32,768]{2,1,0:T(8,128)(2,1)S(1)}, bf16[2,32,768]{2,1,0:T(8,128)(2,1)S(1)}, f32[4,16,9,2,128]{4,3,2,1,0:T(2,128)S(1)}) custom-call(bf16[2,32,768]{2,1,0:T(8,128)(2,1)S(1)} %get-tuple-element.16.refs_0_, bf16[2,32,768]{2,1,0:T(8,128)(2,1)S(1)} %get-tuple-element.15.refs_1_, bf16[3,3,32,512]{3,2,1,0:T(8,128)(2,1)S(1)} %bitcast.8), custom_call_target="tpu_custom_call" | custom-call | tf_op jit(solution)/shard_map/conv_all/pallas_call | solution.py:512
  50.8 1.0 %finish.1 = (bf16[32,2,768]{2,1,0:T(2,128)(2,1)}, bf16[32,2,768]{2,1,0:T(2,128)(2,1)}, f32[9,32,512]{2,1,0:T(8,128)}) custom-call(bf16[2,32,768]{2,1,0:T(8,128)(2,1)S(1)} %get-tuple-element.9.conv_in, bf16[2,32,768]{2,1,0:T(8,128)(2,1)S(1)} %get-tuple-element.10.grad_in, f32[4,16,9,2,128]{4,3,2,1,0:T(2,128)S(1)} %get-tuple-element.11.blocks), custom_call_target="tpu_custom_call" | custom-call | tf_op jit(solution)/shard_map/finish/pallas_call | solution.py:554
Async XLA Ops:
  0.6 1.1 %copy-start = (bf16[32,3,3,512]{3,0,2,1:T(8,128)(2,1)S(1)}, bf16[32,3,3,512]{3,0,2,1:T(8,128)(2,1)}, u32[]{:S(2)}) copy-start(bf16[32,3,3,512]{3,0,2,1:T(8,128)(2,1)} %param.4) | copy-start | bytes 884740

commit v5 on v4

--- a/solution.py
+++ b/solution.py
@@ -101,6 +101,7 @@
 IDS = [message_ids(stages) for stages in PLANS]
 N_MSG = 32
 Z_ORDER = [4, 3, 5, 2, 6, 1, 7]
+FAR_FIRST = [(y, x, c) for y in (2, 1, 3, 0) for x in (1, 0) for c in (1, 0) if (y, x, c) != (0, 0, 0)]
 BOTH = (2,)
 
 
@@ -160,13 +161,11 @@
         return y * 4 + x * 2 + c
 
     barrier = pltpu.get_barrier_semaphore()
-    for d in range(1, 16):
-        pl.semaphore_signal(
-            barrier, inc=1, device_id={"chan": lax.rem(k + d, 16)}, device_id_type=MESH
-        )
-    near_width = [lax.rem(w + 2 * d, n_width) for d in range(1, n_z)] + [right, left]
+    near_width = [lax.rem(w + 2 * d, n_width) for d in Z_ORDER] + [right, left]
     for device in near_width:
         pl.semaphore_signal(barrier, inc=1, device_id={"width": device}, device_id_type=MESH)
+    for way in FAR_FIRST:
+        pl.semaphore_signal(barrier, inc=1, device_id={"chan": chan_of(*way)}, device_id_type=MESH)
 
     def own_rows(index):
         return pl.ds(pl.multiple_of(index * 32, 32), 32)

time: 51.9 us -> 51.8 us (level)
  no operation moved by 1% of the time
where the time goes in v5:
time: 51.8 us; the launch traced here: 51.7 us
  Pallas kernels  50 us (97%)
  local copies, waits for them, and re-layouts  1.05 us (2%)
  between operations  0.65 us (1%)
    pallas_call x1, Pallas kernels, body(): pl.pallas_call(run, out_shape=[jax.ShapeDtypeStruct((rows, cin_dev, cols)...  49 us

profile of v5, /device:TPU:4, one launch (start us, length us, event | category | flops | bytes accessed | tf_op | source)
XLA Modules:
  0.0 51.7 jit_solution(11583926374805790576)
XLA Ops:
  0.6 0.0 copy-start
  0.6 1.0 %copy_bitcast_fusion = (bf16[2,32,768]{2,1,0:T(8,128)(2,1)S(1)}, bf16[2,32,768]{2,1,0:T(8,128)(2,1)S(1)}) fusion(bf16[32,2,768]{2,1,0:T(2,128)(2,1)} %param.5, bf16[32,2,768]{2,1,0:T(2,128)(2,1)} %param.3), kind=kLoop, calls=%fused_computation | loop fusion | bytes 393216 | tf_op jit(solution)/shard_map/transpose | solution.py:503
  1.6 0.0 copy-done
  1.7 49.0 %conv_all.1 = (bf16[2,32,768]{2,1,0:T(8,128)(2,1)S(1)}, bf16[2,32,768]{2,1,0:T(8,128)(2,1)S(1)}, f32[4,16,9,2,128]{4,3,2,1,0:T(2,128)S(1)}) custom-call(bf16[2,32,768]{2,1,0:T(8,128)(2,1)S(1)} %get-tuple-element.16.refs_0_, bf16[2,32,768]{2,1,0:T(8,128)(2,1)S(1)} %get-tuple-element.15.refs_1_, bf16[3,3,32,512]{3,2,1,0:T(8,128)(2,1)S(1)} %bitcast.8), custom_call_target="tpu_custom_call" | custom-call | tf_op jit(solution)/shard_map/conv_all/pallas_call | solution.py:511
  50.7 1.0 %finish.1 = (bf16[32,2,768]{2,1,0:T(2,128)(2,1)}, bf16[32,2,768]{2,1,0:T(2,128)(2,1)}, f32[9,32,512]{2,1,0:T(8,128)}) custom-call(bf16[2,32,768]{2,1,0:T(8,128)(2,1)S(1)} %get-tuple-element.9.conv_in, bf16[2,32,768]{2,1,0:T(8,128)(2,1)S(1)} %get-tuple-element.10.grad_in, f32[4,16,9,2,128]{4,3,2,1,0:T(2,128)S(1)} %get-tuple-element.11.blocks), custom_call_target="tpu_custom_call" | custom-call | tf_op jit(solution)/shard_map/finish/pallas_call | solution.py:553
Async XLA Ops:
  0.6 1.1 %copy-start = (bf16[32,3,3,512]{3,0,2,1:T(8,128)(2,1)S(1)}, bf16[32,3,3,512]{3,0,2,1:T(8,128)(2,1)}, u32[]{:S(2)}) copy-start(bf16[32,3,3,512]{3,0,2,1:T(8,128)(2,1)} %param.4) | copy-start | bytes 884740

commit v6 on v5

--- a/solution.py
+++ b/solution.py
@@ -389,8 +389,8 @@
     for d in range(1, 16):
         start(f_copy(d))
     sum_along_z(1)
+    sum_along_z(3)
     hand_out(0)
-    sum_along_z(3)
     gather_stage(1, 2)
 
     lane32 = lax.broadcasted_iota(jnp.int32, (32, cols), 1)

time: 51.8 us -> 51.7 us (level)
  no operation moved by 1% of the time
where the time goes in v6:
time: 51.7 us; the launch traced here: 51.6 us
  Pallas kernels  49.9 us (97%)
  local copies, waits for them, and re-layouts  1.05 us (2%)
  between operations  0.65 us (1%)
    pallas_call x1, Pallas kernels, body(): pl.pallas_call(run, out_shape=[jax.ShapeDtypeStruct((rows, cin_dev, cols)...  48.9 us

profile of v6, /device:TPU:4, one launch (start us, length us, event | category | flops | bytes accessed | tf_op | source)
XLA Modules:
  0.0 51.6 jit_solution(5336412300996655518)
XLA Ops:
  0.6 0.0 copy-start
  0.6 1.0 %copy_bitcast_fusion = (bf16[2,32,768]{2,1,0:T(8,128)(2,1)S(1)}, bf16[2,32,768]{2,1,0:T(8,128)(2,1)S(1)}) fusion(bf16[32,2,768]{2,1,0:T(2,128)(2,1)} %param.5, bf16[32,2,768]{2,1,0:T(2,128)(2,1)} %param.3), kind=kLoop, calls=%fused_computation | loop fusion | bytes 393216 | tf_op jit(solution)/shard_map/transpose | solution.py:503
  1.6 0.0 copy-done
  1.7 48.9 %conv_all.1 = (bf16[2,32,768]{2,1,0:T(8,128)(2,1)S(1)}, bf16[2,32,768]{2,1,0:T(8,128)(2,1)S(1)}, f32[4,16,9,2,128]{4,3,2,1,0:T(2,128)S(1)}) custom-call(bf16[2,32,768]{2,1,0:T(8,128)(2,1)S(1)} %get-tuple-element.16.refs_0_, bf16[2,32,768]{2,1,0:T(8,128)(2,1)S(1)} %get-tuple-element.15.refs_1_, bf16[3,3,32,512]{3,2,1,0:T(8,128)(2,1)S(1)} %bitcast.8), custom_call_target="tpu_custom_call" | custom-call | tf_op jit(solution)/shard_map/conv_all/pallas_call | solution.py:511
  50.6 1.0 %finish.1 = (bf16[32,2,768]{2,1,0:T(2,128)(2,1)}, bf16[32,2,768]{2,1,0:T(2,128)(2,1)}, f32[9,32,512]{2,1,0:T(8,128)}) custom-call(bf16[2,32,768]{2,1,0:T(8,128)(2,1)S(1)} %get-tuple-element.9.conv_in, bf16[2,32,768]{2,1,0:T(8,128)(2,1)S(1)} %get-tuple-element.10.grad_in, f32[4,16,9,2,128]{4,3,2,1,0:T(2,128)S(1)} %get-tuple-element.11.blocks), custom_call_target="tpu_custom_call" | custom-call | tf_op jit(solution)/shard_map/finish/pallas_call | solution.py:553
Async XLA Ops:
  0.6 1.1 %copy-start = (bf16[32,3,3,512]{3,0,2,1:T(8,128)(2,1)S(1)}, bf16[32,3,3,512]{3,0,2,1:T(8,128)(2,1)}, u32[]{:S(2)}) copy-start(bf16[32,3,3,512]{3,0,2,1:T(8,128)(2,1)} %param.4) | copy-start | bytes 884740
